TPU v7x, 32 devices: a whole 2x2x4 slice. The times are simulated.
32 devices in a mesh: grid: 8 (over z, core), tp: 4 (over y, x).
Axes of the slice: x: 2, y: 2, z: 4, core: 2. Of those that a mesh axis runs over, the one named last changes fastest.
Arguments:
- latents: bfloat16 [3072, 3072], P('grid'), may hold values from -6 to 6
- input_weight: bfloat16 [3072, 1536], P('grid', 'tp'), as said below
- norm_gains: float32 [2, 128], replicated, as said below
- text_pairs: bfloat16 [256, 1024], P(None, 'tp'), may hold values from -6 to 6
- text_count: int32 [1], replicated, may hold values from 64 to 256
- output_weight: bfloat16 [512, 3072], P('tp', 'grid'), may hold values from -0.25 to 0.25
Outputs:
- block_output: bfloat16 [3072, 3072], P('grid', 'tp')
Inputs may be any that keep to these rules, and one draw needn't show every extreme that they name: `text_count`: number of valid text tokens; the remaining text slots are padding. `input_weight`: a projection scaled by its fan-in. `norm_gains`: positive gains.
All inputs are finite; a program needn't handle non-finite values.
Results may differ from a plain program's by a relative error of at most 0.015.
Values may be sent and summed in bfloat16 or wider, within the bound.
No kernel may reach another device: no remote copies, remote signals or barrier semaphores. Data moves between devices by JAX's collectives and lax.ppermute only.
A program may use at most 64 MiB of HBM per device.

v0:
```python
import jax
import jax.numpy as jnp
import numpy as np
from jax import lax
from jax.sharding import PartitionSpec as P

GRID_H = 4
TILE = 384
epsilon = 1e-06


def shifted(x, axis, by):
    length = lax.axis_size(axis)
    pairs = [(i, i + by) for i in range(length) if 0 <= i + by < length]
    return lax.ppermute(x, axis, pairs)


def root_norm(values, gain):
    return values * lax.rsqrt(jnp.mean(values * values, axis=-1, keepdims=True) + epsilon) * gain


def local(latents, input_weight, norm_gains, text_pairs, text_count, output_weight):
    row_count = latents.shape[0]
    in_width = input_weight.shape[1]
    head_size = norm_gains.shape[1]
    head_count = in_width // (3 * head_size)
    tile_rows = TILE
    tiles_wide = row_count // tile_rows
    projected = jnp.dot(
        latents,
        lax.all_gather(input_weight, "grid", axis=0, tiled=True),
        preferred_element_type=jnp.float32,
    )
    projected = projected.reshape(row_count, head_count, 3, head_size)
    queries = root_norm(projected[:, :, 0], norm_gains[0]).astype(jnp.bfloat16)
    key_rows = root_norm(projected[:, :, 1], norm_gains[1]).astype(jnp.bfloat16)
    values = projected[:, :, 2].astype(jnp.bfloat16)
    stacked = jnp.concatenate(
        [
            key_rows.reshape(row_count, head_count * head_size),
            values.reshape(row_count, head_count * head_size),
        ],
        axis=1,
    )
    offsets = [(step_time, step_height) for step_time in (-1, 0, 1) for step_height in (-1, 0, 1)]
    neighbours = []
    for step_time, step_height in offsets:
        if step_time == 0 and step_height == 0:
            neighbours.append(stacked)
        else:
            neighbours.append(shifted(stacked, "grid", -(step_time * GRID_H + step_height)))
    planes = jnp.stack(neighbours)
    grid_time = lax.axis_size("grid") // GRID_H
    place = lax.axis_index("grid")
    time_here = place // GRID_H
    height_here = place % GRID_H
    plane_ok = jnp.stack(
        [
            (time_here + step_time >= 0)
            & (time_here + step_time < grid_time)
            & ((height_here + step_height >= 0) & (height_here + step_height < GRID_H))
            for step_time, step_height in offsets
        ]
    )
    width_keep = min(3, tiles_wide)
    starts = np.clip(np.arange(tiles_wide) - 1, 0, tiles_wide - width_keep)
    width_index = starts[:, None] + np.arange(width_keep)[None, :]
    width_ok = np.abs(width_index - np.arange(tiles_wide)[:, None]) <= 1
    window_rows = 9 * width_keep * tile_rows
    planes = planes.reshape(9, tiles_wide, tile_rows, 2 * head_count * head_size)
    window = (
        planes[:, width_index]
        .transpose(1, 0, 2, 3, 4)
        .reshape(tiles_wide, window_rows, 2, head_count, head_size)
    )
    key_window = window[:, :, 0]
    value_window = window[:, :, 1]
    live = plane_ok[None, :, None, None] & jnp.asarray(width_ok)[:, None, :, None]
    live = jnp.broadcast_to(live, (tiles_wide, 9, width_keep, tile_rows)).reshape(
        tiles_wide, window_rows
    )
    text = text_pairs.reshape(text_pairs.shape[0], head_count, 2, head_size)
    text_keys = root_norm(text[:, :, 0].astype(jnp.float32), norm_gains[1]).astype(jnp.bfloat16)
    text_values = text[:, :, 1]
    live_text = jnp.arange(text_pairs.shape[0]) < text_count[0]
    score_scale = head_size ** (-0.5)
    query_tiles = queries.reshape(tiles_wide, tile_rows, head_count, head_size)
    video_scores = (
        jnp.einsum("wqhd,wkhd->whqk", query_tiles, key_window, preferred_element_type=jnp.float32)
        * score_scale
    )
    text_scores = (
        jnp.einsum("wqhd,khd->whqk", query_tiles, text_keys, preferred_element_type=jnp.float32)
        * score_scale
    )
    video_scores = jnp.where(live[:, None, None, :], video_scores, -jnp.inf)
    text_scores = jnp.where(live_text[None, None, None, :], text_scores, -jnp.inf)
    row_max = jnp.maximum(video_scores.max(-1), text_scores.max(-1))[..., None]
    video_exp = jnp.exp(video_scores - row_max)
    text_exp = jnp.exp(text_scores - row_max)
    denominator = video_exp.sum(-1, keepdims=True) + text_exp.sum(-1, keepdims=True)
    video_weights = (video_exp / denominator).astype(jnp.bfloat16)
    text_weights = (text_exp / denominator).astype(jnp.bfloat16)
    mixed = jnp.einsum(
        "whqk,wkhd->wqhd", video_weights, value_window, preferred_element_type=jnp.float32
    )
    mixed = mixed + jnp.einsum(
        "whqk,khd->wqhd", text_weights, text_values, preferred_element_type=jnp.float32
    )
    attention = mixed.astype(jnp.bfloat16).reshape(row_count, head_count * head_size)
    term = jnp.dot(
        attention,
        lax.all_gather(output_weight, "grid", axis=1, tiled=True),
        preferred_element_type=jnp.float32,
    )
    return lax.psum_scatter(term.astype(jnp.bfloat16), "tp", scatter_dimension=1, tiled=True)


def solution(mesh):
    placed = (P("grid", None), P("grid", "tp"), P(), P(None, "tp"), P(), P("tp", "grid"))
    return jax.shard_map(
        local, mesh=mesh, in_specs=placed, out_specs=P("grid", "tp"), check_vma=False
    )
```

profile of v0, /device:TPU:0, one launch (start us, length us, event | category | flops | bytes accessed | tf_op | source)
XLA Modules:
  0.0 153.9 jit_solution(12105154632013553771)
XLA Ops:
  6.5 0.0 copy-start
  6.5 0.0 all-gather.2.cloned.1.call-start
  6.5 0.7 all-gather.2.cloned.1.call-update
  7.3 0.0 reduce-scatter.2.cloned.1.call-start
  7.4 0.1 stack.79
  7.5 0.1 broadcast_in_dim.44
  7.6 1.0 copy.16
  8.6 0.0 copy-start.4
  9.3 0.5 iota_compare_fusion
  9.8 0.8 slice_bitcast_fusion.2
  10.6 0.6 add_rsqrt_fusion.2
  11.2 21.6 %all_gather.7 = bf16[128,3072]{1,0:T(8,128)(2,1)} all-gather(bf16[128,384]{1,0:T(8,128)(2,1)} %param.14), channel_id=1, replica_groups=mesh['grid'=8,'tp'=4] {'grid'}, dimensions={1}, use_global_device_ids=true | all-gather | bytes 884736 | tf_op jit(solution)/shard_map/all_gather | solution.py:113
  32.8 0.0 copy-done.4
  32.8 13.9 %all-gather.2.cloned.1.call-done = bf16[3072,384]{1,0:T(8,128)(2,1)} async-done(((bf16[384,384]{1,0:T(8,128)(2,1)}), bf16[3072,384]{1,0:T(8,128)(2,1)}) %all-gather.2.cloned.1.call-update) | async-done | bytes 2359312 | tf_op jit(solution)/shard_map/all_gather | solution.py:31
  46.6 0.0 copy-done
  46.7 3.1 %fusion.34 = f32[384,384]{0,1:T(8,128)S(1)} fusion(bf16[384,3072]{1,0:T(8,128)(2,1)S(1)} %copy-done, bf16[3072,384]{1,0:T(8,128)(2,1)} %all-gather.2.cloned.1.call-done), kind=kOutput, calls=%fused_computation.61 | convolution fusion | flops 905969664 | bytes 5308416 | tf_op jit(solution)/shard_map/dot_general | solution.py:29
  49.8 0.1 copy.23
  49.9 0.1 multiply_reduce_fusion.1
  50.1 0.1 copy.24
  50.2 0.1 fusion.18
  50.4 3.1 %collective-permute-start = (bf16[384,256]{1,0:T(8,128)(2,1)S(1)}, bf16[384,256]{1,0:T(8,128)(2,1)S(1)}, u32[]{:S(2)}, u32[]{:S(2)}) collective-permute-start(bf16[384,256]{1,0:T(8,128)(2,1)S(1)} %pad_maximum_fusion), channel_id=1, source_target_pairs={{0,20},{4,24},{8,28},{1,21},{5,25},{9,29},{2,22},{6,26},{10,30},{3... | collective-permute-start | bytes 589832 | tf_op jit(solution)/shard_map/ppermute | solution.py:15
  53.5 1.3 collective-permute-start.1
  54.8 2.3 %collective-permute-start.2 = (bf16[384,256]{1,0:T(8,128)(2,1)S(1)}, bf16[384,256]{1,0:T(8,128)(2,1)S(1)}, u32[]{:S(2)}, u32[]{:S(2)}) collective-permute-start(bf16[384,256]{1,0:T(8,128)(2,1)S(1)} %pad_maximum_fusion), channel_id=1, source_target_pairs={{0,12},{4,16},{8,20},{12,24},{16,28},{1,13},{5,17},{9,21},{13,25},... | collective-permute-start | bytes 589832 | tf_op jit(solution)/shard_map/ppermute | solution.py:15
  57.1 1.3 collective-permute-start.3
  58.4 1.3 collective-permute-start.4
  59.7 1.9 %fusion.33 = (f32[384]{0:T(512)S(1)}, f32[1,256,1,384]{3,1,2,0:T(8,128)}) fusion(f32[384,1,3,128]{0,3,2,1:T(8,128)S(1)} %bitcast.111, f32[128]{0:T(128)S(1)} %get-tuple-element.9, f32[384]{0:T(512)S(1)} %add_rsqrt_fusion, f32[128]{0:T(128)S(1)} %get-tuple-element.10, f32[256]{0:T(256)} %add_rsqrt_fusion.2, bf16[256,1,2,128]{0,3,2,1:T(8,128)(2,1)} %bitcast.114, ...), kind=kOutput, calls=%fused_computation.60 | convolution fusion | flops 25738880 | bytes 661504 | tf_op jit(solution)/shard_map/wqhd,khd->whqk/dot_general | solution.py:93
  61.6 0.0 collective-permute-done
  61.6 1.3 collective-permute-start.5
  62.9 0.7 bitcast_dynamic-update-slice_fusion.8
  63.6 0.0 collective-permute-done.1
  63.6 1.3 collective-permute-start.6
  64.9 0.7 bitcast_dynamic-update-slice_fusion.7
  65.6 1.6 %collective-permute-done.2 = bf16[384,256]{1,0:T(8,128)(2,1)S(1)} collective-permute-done((bf16[384,256]{1,0:T(8,128)(2,1)S(1)}, bf16[384,256]{1,0:T(8,128)(2,1)S(1)}, u32[]{:S(2)}, u32[]{:S(2)}) %collective-permute-start.2) | collective-permute-done | bytes 196640 | tf_op jit(solution)/shard_map/ppermute | solution.py:15
  67.2 1.3 collective-permute-start.7
  68.5 0.7 bitcast_dynamic-update-slice_fusion.6
  69.2 0.0 collective-permute-done.3
  69.2 0.7 bitcast_dynamic-update-slice_fusion.5
  69.9 0.7 bitcast_dynamic-update-slice_fusion.4
  70.6 0.0 collective-permute-done.4
  70.6 0.7 bitcast_dynamic-update-slice_fusion.3
  71.3 0.0 collective-permute-done.5
  71.3 0.7 bitcast_dynamic-update-slice_fusion.2
  72.0 6.6 %collective-permute-done.6 = bf16[384,256]{1,0:T(8,128)(2,1)S(1)} collective-permute-done((bf16[384,256]{1,0:T(8,128)(2,1)S(1)}, bf16[384,256]{1,0:T(8,128)(2,1)S(1)}, u32[]{:S(2)}, u32[]{:S(2)}) %collective-permute-start.6) | collective-permute-done | bytes 196640 | tf_op jit(solution)/shard_map/ppermute | solution.py:15
  78.6 0.7 bitcast_dynamic-update-slice_fusion.1
  79.3 10.5 %collective-permute-done.7 = bf16[384,256]{1,0:T(8,128)(2,1)S(1)} collective-permute-done((bf16[384,256]{1,0:T(8,128)(2,1)S(1)}, bf16[384,256]{1,0:T(8,128)(2,1)S(1)}, u32[]{:S(2)}, u32[]{:S(2)}) %collective-permute-start.7) | collective-permute-done | bytes 196640 | tf_op jit(solution)/shard_map/ppermute | solution.py:15
  89.8 0.7 bitcast_dynamic-update-slice_fusion
  90.5 4.5 %reshape_transpose.3 = bf16[1,3456,2,1,128]{4,2,1,3,0:T(2,128)(2,1)} reshape(bf16[9,384,256]{2,1,0:T(8,128)(2,1)} %bitcast_dynamic-update-slice_fusion) | data formatting | bytes 3538944 | tf_op jit(solution)/shard_map/reshape;transpose | solution.py:74
  95.0 5.8 %fusion.30 = (bf16[1,3456,1,1,128]{4,2,1,3,0:T(2,128)(2,1)}, bf16[1,3456,1,1,128]{4,2,1,3,0:T(2,128)(2,1)S(1)}) fusion(bf16[1,3456,2,1,128]{4,2,1,3,0:T(2,128)(2,1)} %reshape_transpose.3), kind=kLoop, calls=%fused_computation.57 | loop fusion | bytes 3538944 | tf_op jit(solution)/shard_map/slice | solution.py:77
  100.8 0.0 copy-start.3
  100.8 1.1 fusion.32
  101.9 0.0 copy-start.1
  101.9 0.0 copy-done.3
  102.0 0.1 fusion.15
  102.1 0.0 copy-start.5
  102.1 0.0 copy-start.2
  102.1 0.9 fusion.1
  102.9 1.3 copy-done.1
  104.3 0.0 copy-done.5
  104.3 0.2 convolution_bitcast_fusion
  104.5 0.0 copy-done.2
  104.5 6.8 %convolution_convert_fusion = bf16[384,3072]{1,0:T(8,128)(2,1)} fusion(bf16[128,3072]{1,0:T(8,128)(2,1)S(1)} %copy-done.2, f32[1,384,1,128]{1,3,2,0:T(8,128)S(1)} %convolution_bitcast_fusion, f32[384,3456]{1,0:T(8,128)} %copy-done.1, f32[384]{0:T(512)S(1)} %add.90, f32[384]{0:T(512)S(1)} %max.9, bf16[1,3456,1,1,128]{4,2,1,3,0:T(2,128)(2,1)} %get-tuple-element.5), kind=kOutput, calls=%fused_computation.5 | convolution fusion | flops 646987776 | bytes 9538560 | tf_op jit(solution)/shard_map/dot_general | solution.py:111
  111.3 0.0 reduce-scatter.2.cloned.1.call-update
  111.3 35.7 %reduce-scatter.2.cloned.1.call-done = bf16[384,768]{1,0:T(8,128)(2,1)} async-done(((bf16[384,3072]{1,0:T(8,128)(2,1)}), bf16[384,768]{1,0:T(8,128)(2,1)}) %reduce-scatter.2.cloned.1.call-update) | async-done | bytes 589840 | tf_op jit(solution)/shard_map/reduce_scatter | solution.py:116
  (9 shorter events, 0.2 us)
Async XLA Ops:
  6.5 40.1 %copy-start = (bf16[384,3072]{1,0:T(8,128)(2,1)S(1)}, bf16[384,3072]{1,0:T(8,128)(2,1)}, u32[]{:S(2)}) copy-start(bf16[384,3072]{1,0:T(8,128)(2,1)} %param.9) | copy-start | bytes 7077892
  6.5 40.1 %all-gather.2.cloned.1.call-start = ((), (), s32[]{:S(2)}) async-start(), calls=%async_computation.1 | async-start | bytes 2654208 | tf_op jit(solution)/shard_map/all_gather | solution.py:31
  7.3 139.8 %reduce-scatter.2.cloned.1.call-start = ((), (), s32[]{:S(2)}) async-start(), calls=%async_computation.2 | async-start | bytes 2949120 | tf_op jit(solution)/shard_map/reduce_scatter | solution.py:116
  8.6 24.2 %copy-start.4 = (bf16[256,256]{0,1:T(8,128)(2,1)}, bf16[256,256]{0,1:T(8,128)(2,1)S(1)}, u32[]{:S(2)}) copy-start(bf16[256,256]{0,1:T(8,128)(2,1)S(1)} %copy.16) | copy-start | bytes 393220
  50.4 11.3 %collective-permute-start = (bf16[384,256]{1,0:T(8,128)(2,1)S(1)}, bf16[384,256]{1,0:T(8,128)(2,1)S(1)}, u32[]{:S(2)}, u32[]{:S(2)}) collective-permute-start(bf16[384,256]{1,0:T(8,128)(2,1)S(1)} %pad_maximum_fusion), channel_id=1, source_target_pairs={{0,20},{4,24},{8,28},{1,21},{5,25},{9,29},{2,22},{6,26},{10,30},{3... | collective-permute-start | bytes 589832 | tf_op jit(solution)/shard_map/ppermute | solution.py:15
  53.5 10.1 %collective-permute-start.1 = (bf16[384,256]{1,0:T(8,128)(2,1)S(1)}, bf16[384,256]{1,0:T(8,128)(2,1)S(1)}, u32[]{:S(2)}, u32[]{:S(2)}) collective-permute-start(bf16[384,256]{1,0:T(8,128)(2,1)S(1)} %pad_maximum_fusion), channel_id=1, source_target_pairs={{0,16},{4,20},{8,24},{12,28},{1,17},{5,21},{9,25},{13,29},{2,18},{... | collective-permute-start | bytes 589832 | tf_op jit(solution)/shard_map/ppermute | solution.py:15
  54.8 12.4 %collective-permute-start.2 = (bf16[384,256]{1,0:T(8,128)(2,1)S(1)}, bf16[384,256]{1,0:T(8,128)(2,1)S(1)}, u32[]{:S(2)}, u32[]{:S(2)}) collective-permute-start(bf16[384,256]{1,0:T(8,128)(2,1)S(1)} %pad_maximum_fusion), channel_id=1, source_target_pairs={{0,12},{4,16},{8,20},{12,24},{16,28},{1,13},{5,17},{9,21},{13,25},... | collective-permute-start | bytes 589832 | tf_op jit(solution)/shard_map/ppermute | solution.py:15
  57.1 12.1 %collective-permute-start.3 = (bf16[384,256]{1,0:T(8,128)(2,1)S(1)}, bf16[384,256]{1,0:T(8,128)(2,1)S(1)}, u32[]{:S(2)}, u32[]{:S(2)}) collective-permute-start(bf16[384,256]{1,0:T(8,128)(2,1)S(1)} %pad_maximum_fusion), channel_id=1, source_target_pairs={{0,4},{4,8},{8,12},{12,16},{16,20},{20,24},{24,28},{1,5},{5,9},{9,... | collective-permute-start | bytes 589832 | tf_op jit(solution)/shard_map/ppermute | solution.py:15
  58.4 12.2 %collective-permute-start.4 = (bf16[384,256]{1,0:T(8,128)(2,1)S(1)}, bf16[384,256]{1,0:T(8,128)(2,1)S(1)}, u32[]{:S(2)}, u32[]{:S(2)}) collective-permute-start(bf16[384,256]{1,0:T(8,128)(2,1)S(1)} %pad_maximum_fusion), channel_id=1, source_target_pairs={{4,0},{8,4},{12,8},{16,12},{20,16},{24,20},{28,24},{5,1},{9,5},{13... | collective-permute-start | bytes 589832 | tf_op jit(solution)/shard_map/ppermute | solution.py:15
  61.6 9.6 %collective-permute-start.5 = (bf16[384,256]{1,0:T(8,128)(2,1)S(1)}, bf16[384,256]{1,0:T(8,128)(2,1)S(1)}, u32[]{:S(2)}, u32[]{:S(2)}) collective-permute-start(bf16[384,256]{1,0:T(8,128)(2,1)S(1)} %pad_maximum_fusion), channel_id=1, source_target_pairs={{12,0},{16,4},{20,8},{24,12},{28,16},{13,1},{17,5},{21,9},{25,13},... | collective-permute-start | bytes 589832 | tf_op jit(solution)/shard_map/ppermute | solution.py:15
  63.6 15.0 %collective-permute-start.6 = (bf16[384,256]{1,0:T(8,128)(2,1)S(1)}, bf16[384,256]{1,0:T(8,128)(2,1)S(1)}, u32[]{:S(2)}, u32[]{:S(2)}) collective-permute-start(bf16[384,256]{1,0:T(8,128)(2,1)S(1)} %pad_maximum_fusion), channel_id=1, source_target_pairs={{16,0},{20,4},{24,8},{28,12},{17,1},{21,5},{25,9},{29,13},{18,2},{... | collective-permute-start | bytes 589832 | tf_op jit(solution)/shard_map/ppermute | solution.py:15
  67.2 22.6 %collective-permute-start.7 = (bf16[384,256]{1,0:T(8,128)(2,1)S(1)}, bf16[384,256]{1,0:T(8,128)(2,1)S(1)}, u32[]{:S(2)}, u32[]{:S(2)}) collective-permute-start(bf16[384,256]{1,0:T(8,128)(2,1)S(1)} %pad_maximum_fusion), channel_id=1, source_target_pairs={{20,0},{24,4},{28,8},{21,1},{25,5},{29,9},{22,2},{26,6},{30,10},{2... | collective-permute-start | bytes 589832 | tf_op jit(solution)/shard_map/ppermute | solution.py:15
  100.8 1.1 copy-start.3
  101.9 2.3 %copy-start.1 = (f32[384,3456]{1,0:T(8,128)}, f32[384,3456]{1,0:T(8,128)S(1)}, u32[]{:S(2)}) copy-start(f32[384,3456]{1,0:T(8,128)S(1)} %get-tuple-element.12) | copy-start | bytes 15925252
  102.1 2.2 %copy-start.5 = (bf16[256,256]{0,1:T(8,128)(2,1)S(1)}, bf16[256,256]{0,1:T(8,128)(2,1)}, u32[]{:S(2)}) copy-start(bf16[256,256]{0,1:T(8,128)(2,1)} %copy-done.4) | copy-start | bytes 393220
  102.1 2.4 %copy-start.2 = (bf16[128,3072]{1,0:T(8,128)(2,1)S(1)}, bf16[128,3072]{1,0:T(8,128)(2,1)}, u32[]{:S(2)}) copy-start(bf16[128,3072]{1,0:T(8,128)(2,1)} %all_gather.7) | copy-start | bytes 2359300
Sparse Core Ops, SparseCore 0:
  9.0 37.6 all-gather.1
  111.4 35.5 reduce-scatter.1
where the time goes:
time: 154 us
  waiting for transfers between devices  69.1 us (45%)
  blocking collectives  21.6 us (14%)
  local copies, waits for them, and re-layouts  19.4 us (13%)
  between operations  14.3 us (9%)
  starting transfers between devices  13.2 us (9%)
  matrix products  13.1 us (9%)
  other arithmetic  3.13 us (2%)
    reduce_scatter x1, waiting for transfers between devices, local(): lax.psum_scatter(term.astype(jnp.bfloat16), 'tp', scatter_dimension=1, ti...  35.7 us
    all_gather x1, blocking collectives, local(): lax.all_gather(output_weight, 'grid', axis=1, tiled=True)  21.6 us
    ppermute x8, waiting for transfers between devices, shifted(): return lax.ppermute(x, axis, pairs)  18.8 us
    all_gather x1, waiting for transfers between devices, local(): lax.all_gather(input_weight, 'grid', axis=0, tiled=True)  13.9 us
    ppermute x8, starting transfers between devices, shifted(): return lax.ppermute(x, axis, pairs)  13.1 us
    unnamed x22, local copies, waits for them, and re-layouts  7.46 us
    dot_general x1, matrix products, local(): jnp.dot(attention, lax.all_gather(output_weight, 'grid', axis=1, tiled=Tr...  6.76 us
    slice x1, local copies, waits for them, and re-layouts, local(): value_window = window[:, :, 1]  5.84 us
  transfers between devices with their start and end apart: 10, of which 5 were waited for; matrix products, arithmetic and copies ran while one was open for 7% of the time, Pallas kernels for 0%

commit v1 on v0

--- a/solution.py
+++ b/solution.py
@@ -7,6 +7,13 @@
 GRID_H = 4
 TILE = 384
 epsilon = 1e-06
+
+
+def gather_over(x, axis, along):
+    devices = lax.axis_size(axis)
+    parts = jnp.stack([x for _ in range(devices)])
+    parts = lax.all_to_all(parts, axis, split_axis=0, concat_axis=0)
+    return jnp.concatenate(parts, axis=along)
 
 
 def shifted(x, axis, by):
@@ -109,9 +116,7 @@
     )
     attention = mixed.astype(jnp.bfloat16).reshape(row_count, head_count * head_size)
     term = jnp.dot(
-        attention,
-        lax.all_gather(output_weight, "grid", axis=1, tiled=True),
-        preferred_element_type=jnp.float32,
+        attention, gather_over(output_weight, "grid", 1), preferred_element_type=jnp.float32
     )
     return lax.psum_scatter(term.astype(jnp.bfloat16), "tp", scatter_dimension=1, tiled=True)
 

time: 154 us -> 165 us (1.071)
  waiting for transfers between devices: 69.1 us -> 94.3 us
  blocking collectives: 21.6 us -> 0 us
  starting transfers between devices: 13.2 us -> 19.4 us
    all_gather x1, waiting for transfers between devices: 13.9 us -> 39.1 us  [local(): lax.all_gather(input_weight, 'grid', axis=0, tiled=True)]
    all_gather x1 -> x0, blocking collectives: 21.6 us -> none  [local(): lax.all_gather(output_weight, 'grid', axis=1, tiled=True)]
    all_to_all x0 -> x1, starting transfers between devices: none -> 6.35 us  [gather_over(): parts = lax.all_to_all(parts, axis, split_axis=0, concat_axis=0)]
    unnamed x22 -> x25, local copies, waits for them, and re-layouts: 7.46 us -> 7.68 us
  transfers between devices with their start and end apart: 10 -> 11, of which waited for: 5 -> 5; matrix products, arithmetic and copies ran while one was open for 7% -> 17% of each run, Pallas kernels for 0% -> 0%
where the time goes in v1:
time: 165 us; the launch traced here: 164 us
  waiting for transfers between devices  94.3 us (57%)
  local copies, waits for them, and re-layouts  19.9 us (12%)
  starting transfers between devices  19.4 us (12%)
  between operations  14.3 us (9%)
  matrix products  13.2 us (8%)
  other arithmetic  3.2 us (2%)
    all_gather x1, waiting for transfers between devices, local(): lax.all_gather(input_weight, 'grid', axis=0, tiled=True)  39.1 us
    reduce_scatter x1, waiting for transfers between devices, local(): lax.psum_scatter(term.astype(jnp.bfloat16), 'tp', scatter_dimension=1, ti...  35.7 us
    ppermute x8, waiting for transfers between devices, shifted(): return lax.ppermute(x, axis, pairs)  18.7 us
    ppermute x8, starting transfers between devices, shifted(): return lax.ppermute(x, axis, pairs)  13 us
    unnamed x25, local copies, waits for them, and re-layouts  7.68 us
    dot_general x1, matrix products, local(): jnp.dot(attention, gather_over(output_weight, 'grid', 1), preferred_eleme...  6.9 us
    all_to_all x1, starting transfers between devices, gather_over(): parts = lax.all_to_all(parts, axis, split_axis=0, concat_axis=0)  6.35 us
    slice x1, local copies, waits for them, and re-layouts, local(): value_window = window[:, :, 1]  5.84 us
  transfers between devices with their start and end apart: 11, of which 5 were waited for; matrix products, arithmetic and copies ran while one was open for 17% of the time, Pallas kernels for 0%

profile of v1, /device:TPU:0, one launch (start us, length us, event | category | flops | bytes accessed | tf_op | source)
XLA Modules:
  0.0 164.4 jit_solution(2568156918180116861)
XLA Ops:
  6.5 0.0 copy-start
  6.5 0.0 copy-start.5
  6.5 0.0 copy-start.6
  6.5 0.0 all-gather.2.cloned.1.call-start
  6.5 0.7 all-gather.2.cloned.1.call-update
  7.3 1.1 copy.21
  8.3 1.0 stack.91
  9.4 6.4 %all-to-all-start = ((bf16[8,128,384]{1,2,0:T(8,128)(2,1)}), bf16[8,128,384]{1,2,0:T(8,128)(2,1)}, u32[]{:S(2)}, u32[]{:S(2)}) async-start(bf16[8,128,384]{1,2,0:T(8,128)(2,1)} %stack.91), calls=%async_computation | async-start | bytes 1572864 | tf_op jit(solution)/shard_map/all_to_all | solution.py:15
  15.7 0.0 reduce-scatter.2.cloned.1.call-start
  15.8 0.1 stack.90
  15.9 0.1 broadcast_in_dim.44
  16.0 0.0 copy-done.5
  16.0 0.1 copy.17
  16.2 0.0 copy-start.3
  16.8 0.6 iota_compare_fusion
  17.4 0.0 copy-done.6
  17.4 0.6 add_rsqrt_fusion.2
  18.0 0.0 copy-done.3
  18.0 39.1 %all-gather.2.cloned.1.call-done = bf16[3072,384]{1,0:T(8,128)(2,1)} async-done(((bf16[384,384]{1,0:T(8,128)(2,1)}), bf16[3072,384]{1,0:T(8,128)(2,1)}) %all-gather.2.cloned.1.call-update) | async-done | bytes 2359312 | tf_op jit(solution)/shard_map/all_gather | solution.py:38
  57.1 0.0 copy-done
  57.1 3.1 %fusion.34 = f32[384,384]{0,1:T(8,128)S(1)} fusion(bf16[384,3072]{1,0:T(8,128)(2,1)S(1)} %copy-done, bf16[3072,384]{1,0:T(8,128)(2,1)} %all-gather.2.cloned.1.call-done), kind=kOutput, calls=%fused_computation.61 | convolution fusion | flops 905969664 | bytes 5308416 | tf_op jit(solution)/shard_map/dot_general | solution.py:36
  60.3 0.1 copy.25
  60.4 0.1 multiply_reduce_fusion.1
  60.6 0.1 copy.26
  60.7 0.1 fusion.18
  60.9 2.0 %collective-permute-start = (bf16[384,256]{1,0:T(8,128)(2,1)S(1)}, bf16[384,256]{1,0:T(8,128)(2,1)S(1)}, u32[]{:S(2)}, u32[]{:S(2)}) collective-permute-start(bf16[384,256]{1,0:T(8,128)(2,1)S(1)} %pad_maximum_fusion), channel_id=1, source_target_pairs={{0,20},{4,24},{8,28},{1,21},{5,25},{9,29},{2,22},{6,26},{10,30},{3... | collective-permute-start | bytes 589832 | tf_op jit(solution)/shard_map/ppermute | solution.py:22
  62.9 1.3 collective-permute-start.1
  64.2 3.2 %collective-permute-start.2 = (bf16[384,256]{1,0:T(8,128)(2,1)S(1)}, bf16[384,256]{1,0:T(8,128)(2,1)S(1)}, u32[]{:S(2)}, u32[]{:S(2)}) collective-permute-start(bf16[384,256]{1,0:T(8,128)(2,1)S(1)} %pad_maximum_fusion), channel_id=1, source_target_pairs={{0,12},{4,16},{8,20},{12,24},{16,28},{1,13},{5,17},{9,21},{13,25},... | collective-permute-start | bytes 589832 | tf_op jit(solution)/shard_map/ppermute | solution.py:22
  67.4 1.3 collective-permute-start.3
  68.8 1.3 collective-permute-start.4
  70.1 1.9 %fusion.33 = (f32[384]{0:T(512)S(1)}, f32[1,256,1,384]{3,1,2,0:T(8,128)}) fusion(f32[384,1,3,128]{0,3,2,1:T(8,128)S(1)} %bitcast.114, f32[128]{0:T(128)S(1)} %get-tuple-element.9, f32[384]{0:T(512)S(1)} %add_rsqrt_fusion, f32[128]{0:T(128)S(1)} %get-tuple-element.10, f32[256]{0:T(256)} %add_rsqrt_fusion.2, bf16[256,1,2,128]{0,3,2,1:T(8,128)(2,1)} %bitcast.117, ...), kind=kOutput, calls=%fused_computation.60 | convolution fusion | flops 25738880 | bytes 661504 | tf_op jit(solution)/shard_map/wqhd,khd->whqk/dot_general | solution.py:100
  72.0 0.0 collective-permute-done
  72.0 1.3 collective-permute-start.5
  73.3 0.7 bitcast_dynamic-update-slice_fusion.8
  74.0 0.0 collective-permute-done.1
  74.0 1.3 collective-permute-start.6
  75.3 0.7 bitcast_dynamic-update-slice_fusion.7
  76.0 0.1 collective-permute-done.2
  76.0 1.3 collective-permute-start.7
  77.3 0.7 bitcast_dynamic-update-slice_fusion.6
  78.0 0.0 collective-permute-done.3
  78.0 0.7 bitcast_dynamic-update-slice_fusion.5
  78.7 0.7 bitcast_dynamic-update-slice_fusion.4
  79.4 0.0 collective-permute-done.4
  79.4 0.7 bitcast_dynamic-update-slice_fusion.3
  80.1 0.0 collective-permute-done.5
  80.1 0.7 bitcast_dynamic-update-slice_fusion.2
  80.8 5.6 %collective-permute-done.6 = bf16[384,256]{1,0:T(8,128)(2,1)S(1)} collective-permute-done((bf16[384,256]{1,0:T(8,128)(2,1)S(1)}, bf16[384,256]{1,0:T(8,128)(2,1)S(1)}, u32[]{:S(2)}, u32[]{:S(2)}) %collective-permute-start.6) | collective-permute-done | bytes 196640 | tf_op jit(solution)/shard_map/ppermute | solution.py:22
  86.4 0.7 bitcast_dynamic-update-slice_fusion.1
  87.1 13.1 %collective-permute-done.7 = bf16[384,256]{1,0:T(8,128)(2,1)S(1)} collective-permute-done((bf16[384,256]{1,0:T(8,128)(2,1)S(1)}, bf16[384,256]{1,0:T(8,128)(2,1)S(1)}, u32[]{:S(2)}, u32[]{:S(2)}) %collective-permute-start.7) | collective-permute-done | bytes 196640 | tf_op jit(solution)/shard_map/ppermute | solution.py:22
  100.2 0.7 bitcast_dynamic-update-slice_fusion
  100.9 4.5 %reshape_transpose.3 = bf16[1,3456,2,1,128]{4,2,1,3,0:T(2,128)(2,1)} reshape(bf16[9,384,256]{2,1,0:T(8,128)(2,1)} %bitcast_dynamic-update-slice_fusion) | data formatting | bytes 3538944 | tf_op jit(solution)/shard_map/reshape;transpose | solution.py:81
  105.3 5.8 %fusion.30 = (bf16[1,3456,1,1,128]{4,2,1,3,0:T(2,128)(2,1)}, bf16[1,3456,1,1,128]{4,2,1,3,0:T(2,128)(2,1)S(1)}) fusion(bf16[1,3456,2,1,128]{4,2,1,3,0:T(2,128)(2,1)} %reshape_transpose.3), kind=kLoop, calls=%fused_computation.57 | loop fusion | bytes 3538944 | tf_op jit(solution)/shard_map/slice | solution.py:84
  111.2 1.1 fusion.32
  112.3 0.0 copy-done.2
  112.3 0.1 fusion.15
  112.4 0.9 fusion.1
  113.3 1.3 copy-done.1
  114.6 0.0 copy-done.4
  114.6 0.2 convolution_bitcast_fusion
  114.8 0.0 all-to-all-done
  114.9 6.9 %convolution_convert_fusion = bf16[384,3072]{1,0:T(8,128)(2,1)} fusion(bf16[128,3072]{0,1:T(8,128)(2,1)} %bitcast.38, f32[1,384,1,128]{1,3,2,0:T(8,128)S(1)} %convolution_bitcast_fusion, f32[384,3456]{1,0:T(8,128)} %copy-done.1, f32[384]{0:T(512)S(1)} %add.90, f32[384]{0:T(512)S(1)} %max.9, bf16[1,3456,1,1,128]{4,2,1,3,0:T(2,128)(2,1)} %get-tuple-element.5), kind=kOutput, calls=%fused_computation.5 | convolution fusion | flops 646987776 | bytes 9538560 | tf_op jit(solution)/shard_map/dot_general | solution.py:118
  121.7 0.0 reduce-scatter.2.cloned.1.call-update
  121.8 35.7 %reduce-scatter.2.cloned.1.call-done = bf16[384,768]{1,0:T(8,128)(2,1)} async-done(((bf16[384,3072]{1,0:T(8,128)(2,1)}), bf16[384,768]{1,0:T(8,128)(2,1)}) %reduce-scatter.2.cloned.1.call-update) | async-done | bytes 589840 | tf_op jit(solution)/shard_map/reduce_scatter | solution.py:121
  (13 shorter events, 0.2 us)
Async XLA Ops:
  6.5 50.6 %copy-start = (bf16[384,3072]{1,0:T(8,128)(2,1)S(1)}, bf16[384,3072]{1,0:T(8,128)(2,1)}, u32[]{:S(2)}) copy-start(bf16[384,3072]{1,0:T(8,128)(2,1)} %param.9) | copy-start | bytes 7077892
  6.5 9.5 %copy-start.5 = (bf16[256,256]{1,0:T(8,128)(2,1)S(1)}, bf16[256,256]{1,0:T(8,128)(2,1)}, u32[]{:S(2)}) copy-start(bf16[256,256]{1,0:T(8,128)(2,1)} %param.12) | copy-start | bytes 393220
  6.5 10.9 %copy-start.6 = (f32[2,128]{1,0:T(2,128)S(1)}, f32[2,128]{1,0:T(2,128)}, u32[]{:S(2)}) copy-start(f32[2,128]{1,0:T(2,128)} %param.11) | copy-start | bytes 3076
  6.5 50.6 %all-gather.2.cloned.1.call-start = ((), (), s32[]{:S(2)}) async-start(), calls=%async_computation.2 | async-start | bytes 2654208 | tf_op jit(solution)/shard_map/all_gather | solution.py:38
  9.4 105.5 %all-to-all-start = ((bf16[8,128,384]{1,2,0:T(8,128)(2,1)}), bf16[8,128,384]{1,2,0:T(8,128)(2,1)}, u32[]{:S(2)}, u32[]{:S(2)}) async-start(bf16[8,128,384]{1,2,0:T(8,128)(2,1)} %stack.91), calls=%async_computation | async-start | bytes 1572864 | tf_op jit(solution)/shard_map/all_to_all | solution.py:15
  15.7 141.8 %reduce-scatter.2.cloned.1.call-start = ((), (), s32[]{:S(2)}) async-start(), calls=%async_computation.3 | async-start | bytes 2949120 | tf_op jit(solution)/shard_map/reduce_scatter | solution.py:121
  16.2 1.9 %copy-start.3 = (bf16[256,256]{0,1:T(8,128)(2,1)}, bf16[256,256]{0,1:T(8,128)(2,1)S(1)}, u32[]{:S(2)}) copy-start(bf16[256,256]{0,1:T(8,128)(2,1)S(1)} %copy.17) | copy-start | bytes 393220
  60.9 11.1 %collective-permute-start = (bf16[384,256]{1,0:T(8,128)(2,1)S(1)}, bf16[384,256]{1,0:T(8,128)(2,1)S(1)}, u32[]{:S(2)}, u32[]{:S(2)}) collective-permute-start(bf16[384,256]{1,0:T(8,128)(2,1)S(1)} %pad_maximum_fusion), channel_id=1, source_target_pairs={{0,20},{4,24},{8,28},{1,21},{5,25},{9,29},{2,22},{6,26},{10,30},{3... | collective-permute-start | bytes 589832 | tf_op jit(solution)/shard_map/ppermute | solution.py:22
  62.9 11.0 %collective-permute-start.1 = (bf16[384,256]{1,0:T(8,128)(2,1)S(1)}, bf16[384,256]{1,0:T(8,128)(2,1)S(1)}, u32[]{:S(2)}, u32[]{:S(2)}) collective-permute-start(bf16[384,256]{1,0:T(8,128)(2,1)S(1)} %pad_maximum_fusion), channel_id=1, source_target_pairs={{0,16},{4,20},{8,24},{12,28},{1,17},{5,21},{9,25},{13,29},{2,18},{... | collective-permute-start | bytes 589832 | tf_op jit(solution)/shard_map/ppermute | solution.py:22
  64.2 11.8 %collective-permute-start.2 = (bf16[384,256]{1,0:T(8,128)(2,1)S(1)}, bf16[384,256]{1,0:T(8,128)(2,1)S(1)}, u32[]{:S(2)}, u32[]{:S(2)}) collective-permute-start(bf16[384,256]{1,0:T(8,128)(2,1)S(1)} %pad_maximum_fusion), channel_id=1, source_target_pairs={{0,12},{4,16},{8,20},{12,24},{16,28},{1,13},{5,17},{9,21},{13,25},... | collective-permute-start | bytes 589832 | tf_op jit(solution)/shard_map/ppermute | solution.py:22
  67.4 10.6 %collective-permute-start.3 = (bf16[384,256]{1,0:T(8,128)(2,1)S(1)}, bf16[384,256]{1,0:T(8,128)(2,1)S(1)}, u32[]{:S(2)}, u32[]{:S(2)}) collective-permute-start(bf16[384,256]{1,0:T(8,128)(2,1)S(1)} %pad_maximum_fusion), channel_id=1, source_target_pairs={{0,4},{4,8},{8,12},{12,16},{16,20},{20,24},{24,28},{1,5},{5,9},{9,... | collective-permute-start | bytes 589832 | tf_op jit(solution)/shard_map/ppermute | solution.py:22
  68.8 10.7 %collective-permute-start.4 = (bf16[384,256]{1,0:T(8,128)(2,1)S(1)}, bf16[384,256]{1,0:T(8,128)(2,1)S(1)}, u32[]{:S(2)}, u32[]{:S(2)}) collective-permute-start(bf16[384,256]{1,0:T(8,128)(2,1)S(1)} %pad_maximum_fusion), channel_id=1, source_target_pairs={{4,0},{8,4},{12,8},{16,12},{20,16},{24,20},{28,24},{5,1},{9,5},{13... | collective-permute-start | bytes 589832 | tf_op jit(solution)/shard_map/ppermute | solution.py:22
  72.0 8.2 %collective-permute-start.5 = (bf16[384,256]{1,0:T(8,128)(2,1)S(1)}, bf16[384,256]{1,0:T(8,128)(2,1)S(1)}, u32[]{:S(2)}, u32[]{:S(2)}) collective-permute-start(bf16[384,256]{1,0:T(8,128)(2,1)S(1)} %pad_maximum_fusion), channel_id=1, source_target_pairs={{12,0},{16,4},{20,8},{24,12},{28,16},{13,1},{17,5},{21,9},{25,13},... | collective-permute-start | bytes 589832 | tf_op jit(solution)/shard_map/ppermute | solution.py:22
  74.0 12.5 %collective-permute-start.6 = (bf16[384,256]{1,0:T(8,128)(2,1)S(1)}, bf16[384,256]{1,0:T(8,128)(2,1)S(1)}, u32[]{:S(2)}, u32[]{:S(2)}) collective-permute-start(bf16[384,256]{1,0:T(8,128)(2,1)S(1)} %pad_maximum_fusion), channel_id=1, source_target_pairs={{16,0},{20,4},{24,8},{28,12},{17,1},{21,5},{25,9},{29,13},{18,2},{... | collective-permute-start | bytes 589832 | tf_op jit(solution)/shard_map/ppermute | solution.py:22
  76.0 24.1 %collective-permute-start.7 = (bf16[384,256]{1,0:T(8,128)(2,1)S(1)}, bf16[384,256]{1,0:T(8,128)(2,1)S(1)}, u32[]{:S(2)}, u32[]{:S(2)}) collective-permute-start(bf16[384,256]{1,0:T(8,128)(2,1)S(1)} %pad_maximum_fusion), channel_id=1, source_target_pairs={{20,0},{24,4},{28,8},{21,1},{25,5},{29,9},{22,2},{26,6},{30,10},{2... | collective-permute-start | bytes 589832 | tf_op jit(solution)/shard_map/ppermute | solution.py:22
  111.2 1.1 copy-start.2
  112.3 2.3 %copy-start.1 = (f32[384,3456]{1,0:T(8,128)}, f32[384,3456]{1,0:T(8,128)S(1)}, u32[]{:S(2)}) copy-start(f32[384,3456]{1,0:T(8,128)S(1)} %get-tuple-element.12) | copy-start | bytes 15925252
  112.4 2.2 %copy-start.4 = (bf16[256,256]{0,1:T(8,128)(2,1)S(1)}, bf16[256,256]{0,1:T(8,128)(2,1)}, u32[]{:S(2)}) copy-start(bf16[256,256]{0,1:T(8,128)(2,1)} %copy-done.3) | copy-start | bytes 393220
Sparse Core Ops, SparseCore 0:
  9.0 48.1 all-gather.1
  121.9 35.5 reduce-scatter.1
